TPU v7x, 512 devices: a whole 4x4x16 slice. The times are simulated.
512 devices in a mesh: replica: 32 (over z, core), tensor: 16 (over x, y).
Axes of the slice: x: 4, y: 4, z: 16, core: 2. Of those that a mesh axis runs over, the one named last changes fastest.
Arguments:
- x_input: bfloat16 [8192, 4096], P('replica', 'tensor'), may hold values from -6 to 6
- z_input: bfloat16 [8192, 4096], P('replica', 'tensor'), may hold values from -6 to 6
- bc_input: bfloat16 [8192, 1024], P('replica'), may hold values from -6 to 6
- dt_raw: float32 [8192, 128], P('replica', 'tensor'), may hold values from -6 to 6
- dt_bias: float32 [128], P('tensor'), may hold values from -3 to -1
- decay_rates: float32 [128], P('tensor'), may hold values from 0.005 to 0.5
- skip_gain: float32 [128], P('tensor'), may hold values from 0.5 to 1.5
- conv_x: float32 [4, 4096], P(None, 'tensor'), may hold values from -3 to 3
- conv_bc: float32 [4, 1024], replicated, may hold values from -3 to 3
- norm_gain: float32 [4096], P('tensor'), may hold values from 0.5 to 1.5
- out_weight: bfloat16 [4096, 4096], P('tensor'), may hold values from -0.09375 to 0.09375
- cached_states: float32 [64, 128, 32, 128], P('replica', 'tensor'), may hold values from -4 to 4
- cached_tail_x: float32 [64, 3, 4096], P('replica', None, 'tensor'), may hold values from -6 to 6
- cached_tail_bc: float32 [64, 3, 1024], P('replica'), may hold values from -6 to 6
- prefix_block: int32 [64], replicated, may hold values from 0 to 63, as said below
- lengths: int32 [64], P('replica'), may hold values from 128 to 128, as said below
Outputs:
- mixed: bfloat16 [8192, 4096], P(('replica', 'tensor'))
- final_states: float32 [64, 128, 32, 128], P('replica', 'tensor')
Inputs may be any that keep to these rules, and one draw needn't show every extreme that they name: A permutation: request q (on replica q // 2) starts from cached block prefix_block[q], which replica prefix_block[q] // 2 holds; every cached block feeds exactly one request. `lengths`: every request's suffix fills all 128 of its slots, so every entry is 128.
All inputs are finite; a program needn't handle non-finite values.
Results may differ from a plain program's by a relative error of at most 0.015.
Values may be sent and summed in bfloat16 or wider, within the bound.
A program may use at most 64 MiB of HBM per device.

v0:
```python
import jax
import jax.numpy as jnp
from jax import lax
from jax.sharding import PartitionSpec as P

HEADS = 128
HEAD_DIM = 32
STATE = 128
GROUPS = 4
highest = lax.Precision.HIGHEST
epsilon = 1e-05


def causal_conv(tail_rows, sequence, kernel):
    joined = jnp.concatenate([tail_rows, sequence], axis=0)
    length = sequence.shape[0]
    total = joined[0:length] * kernel[0][None, :]
    for offset in range(1, kernel.shape[0]):
        total = total + joined[offset : offset + length] * kernel[offset][None, :]
    return jax.nn.silu(total)


def span_scan(inputs, b_heads, c_heads, step_sizes, decay_rates, skip_gain, carry_state):
    logdec = -step_sizes * decay_rates[None, :]
    cumulative = jnp.cumsum(logdec, axis=0)
    count_rows = inputs.shape[0]
    causal = jnp.arange(count_rows)[:, None] >= jnp.arange(count_rows)[None, :]
    cum_heads = jnp.transpose(cumulative)
    differ = cum_heads[:, :, None] - cum_heads[:, None, :]
    decays = jnp.where(causal[None, :, :], jnp.exp(jnp.minimum(differ, 0.0)), 0.0)
    scores = jnp.einsum("ihn,jhn->hij", c_heads, b_heads, precision=highest)
    weights = scores * decays * jnp.transpose(step_sizes)[:, None, :]
    inside = jnp.einsum("hij,jhp->ihp", weights, inputs, precision=highest)
    carried = jnp.exp(cumulative)[:, :, None] * jnp.einsum(
        "ihn,hpn->ihp", c_heads, carry_state, precision=highest
    )
    output = inside + carried + skip_gain[None, :, None] * inputs
    ending = cumulative[-1]
    weigh_in = jnp.exp(ending[None, :] - cumulative) * step_sizes
    new_state = jnp.exp(ending)[:, None, None] * carry_state + jnp.einsum(
        "jh,jhp,jhn->hpn", weigh_in, inputs, b_heads, precision=highest
    )
    return (output, new_state)


def local(
    x_input,
    z_input,
    bc_input,
    dt_raw,
    dt_bias,
    decay_rates,
    skip_gain,
    conv_x,
    conv_bc,
    norm_gain,
    out_weight,
    cached_states,
    cached_tail_x,
    cached_tail_bc,
    prefix_block,
    lengths,
):
    requests = lengths.shape[0]
    local_heads = dt_raw.shape[1]
    tokens_dev = x_input.shape[0]
    slot_len = tokens_dev // requests
    wanted = lax.dynamic_slice_in_dim(prefix_block, lax.axis_index("replica") * requests, requests)
    empty_carry = (
        jnp.zeros_like(cached_states),
        jnp.zeros_like(cached_tail_x),
        jnp.zeros_like(cached_tail_bc),
    )
    pick_pieces = (
        lax.all_gather(cached_states.astype(jnp.bfloat16), "replica", axis=0, tiled=True).astype(
            jnp.float32
        ),
        lax.all_gather(cached_tail_x.astype(jnp.bfloat16), "replica", axis=0, tiled=True).astype(
            jnp.float32
        ),
        lax.all_gather(cached_tail_bc.astype(jnp.bfloat16), "replica", axis=0, tiled=True).astype(
            jnp.float32
        ),
    )
    count_blocks = pick_pieces[0].shape[0]
    inside = (wanted >= 0) & (wanted < count_blocks)
    position = jnp.clip(wanted, 0, count_blocks - 1)
    chosen = []
    for current, piece in zip(empty_carry, pick_pieces):
        taken_rows = jnp.take(piece, position, axis=0)
        in_mask = inside.reshape((requests,) + (1,) * (current.ndim - 1))
        chosen.append(jnp.where(in_mask, taken_rows, current))
    start_states, start_tail_x, start_tail_bc = tuple(chosen)
    head_ids = lax.axis_index("tensor") * local_heads + jnp.arange(local_heads)
    member = ((head_ids // (HEADS // GROUPS))[:, None] == jnp.arange(GROUPS)[None, :]).astype(
        jnp.float32
    )
    live = jnp.arange(slot_len)[None, :] < lengths[:, None]
    outputs = []
    finals = []
    for request in range(requests):
        row_lo = request * slot_len
        row_hi = row_lo + slot_len
        inputs = causal_conv(
            start_tail_x[request], x_input[row_lo:row_hi].astype(jnp.float32), conv_x
        ).reshape(slot_len, local_heads, HEAD_DIM)
        bc_conv = causal_conv(
            start_tail_bc[request], bc_input[row_lo:row_hi].astype(jnp.float32), conv_bc
        )
        b_groups = bc_conv[:, : GROUPS * STATE].reshape(slot_len, GROUPS, STATE)
        c_groups = bc_conv[:, GROUPS * STATE :].reshape(slot_len, GROUPS, STATE)
        b_heads = jnp.einsum("lgn,hg->lhn", b_groups, member, precision=highest)
        c_heads = jnp.einsum("lgn,hg->lhn", c_groups, member, precision=highest)
        step_sizes = jnp.where(
            live[request][:, None], jax.nn.softplus(dt_raw[row_lo:row_hi] + dt_bias[None, :]), 0.0
        )
        carry_state = start_states[request]
        output, carry_state = span_scan(
            inputs, b_heads, c_heads, step_sizes, decay_rates, skip_gain, carry_state
        )
        outputs.append(output.reshape(slot_len, -1))
        finals.append(carry_state)
    outputs = jnp.concatenate(outputs, axis=0)
    final_states = jnp.stack(finals, axis=0)
    gate_vals = outputs * jax.nn.silu(z_input.astype(jnp.float32))
    by_head = gate_vals.reshape(tokens_dev, local_heads, HEAD_DIM)
    head_squares = jnp.sum(by_head * by_head, axis=2)
    partial_sq = jnp.dot(head_squares, member, precision=highest)
    totals = lax.psum(partial_sq, "tensor")
    mean_sq = jnp.dot(totals, jnp.transpose(member), precision=highest) / (
        HEADS * HEAD_DIM // GROUPS
    )
    normed = (by_head * lax.rsqrt(mean_sq + epsilon)[:, :, None]).reshape(
        tokens_dev, -1
    ) * norm_gain[None, :]
    gated = jnp.where(live.reshape(tokens_dev, 1), normed, 0.0).astype(jnp.bfloat16)
    mixed = lax.psum_scatter(
        jnp.dot(gated, out_weight, preferred_element_type=jnp.float32).astype(jnp.bfloat16),
        "tensor",
        scatter_dimension=0,
        tiled=True,
    )
    return (mixed, final_states)


def solution(mesh):
    placed = (
        P("replica", "tensor"),
        P("replica", "tensor"),
        P("replica", None),
        P("replica", "tensor"),
        P("tensor"),
        P("tensor"),
        P("tensor"),
        P(None, "tensor"),
        P(),
        P("tensor"),
        P("tensor", None),
        P("replica", "tensor", None, None),
        P("replica", None, "tensor"),
        P("replica", None, None),
        P(),
        P("replica"),
    )
    return jax.shard_map(
        local,
        mesh=mesh,
        in_specs=placed,
        out_specs=(P(("replica", "tensor"), None), P("replica", "tensor", None, None)),
        check_vma=False,
    )
```

profile of v0, /device:TPU:2, one launch (start us, length us, event | category | flops | bytes accessed | tf_op | source)
XLA Modules:
  0.0 261.4 jit_solution(10844467314238256731)
XLA Ops:
  7.2 1.8 convert_element_type.46
  9.1 1.3 fusion.71
  15.1 37.8 %all_gather.10 = bf16[64,3,1024]{2,1,0:T(4,128)(2,1)S(1)} all-gather(bf16[2,3,1024]{2,1,0:T(4,128)(2,1)S(1)} %copy.87), channel_id=1, replica_groups=mesh['replica'=32,'tensor'=16] {'replica'}, dimensions={0}, use_global_device_ids=true | all-gather | bytes 405504 | tf_op jit(solution)/shard_map/all_gather | solution.py:81
  53.9 1.1 slice_convert_fusion.1
  57.6 27.6 %all_gather.9 = bf16[64,3,256]{2,1,0:T(4,128)(2,1)S(1)} all-gather(bf16[2,3,256]{2,1,0:T(4,128)(2,1)S(1)} %copy.85), channel_id=1, replica_groups=mesh['replica'=32,'tensor'=16] {'replica'}, dimensions={0}, use_global_device_ids=true | all-gather | bytes 101376 | tf_op jit(solution)/shard_map/all_gather | solution.py:78
  85.9 1.6 gather_fusion
  93.1 1.5 copy.93
  95.4 1.5 copy.101
  97.0 1.7 copy.103
  98.7 1.4 exponential_multiply_fusion.1
  100.6 1.4 convolution_bitcast_fusion.3
  102.0 1.3 fusion.1
  103.3 1.6 convolution_bitcast_fusion.7
  104.9 1.4 convolution_bitcast_fusion
  106.7 1.3 fusion
  108.0 1.6 convolution_bitcast_fusion.5
  109.6 6.6 %convert_element_type.47 = f32[64,8,32,128]{3,2,1,0:T(8,128)} convert(bf16[64,8,32,128]{3,2,1,0:T(8,128)(2,1)} %all-gather.2.cloned.1.call-done) | non-fusion elementwise | flops 2097152 | bytes 12582912 | tf_op jit(solution)/shard_map/convert_element_type | solution.py:75
  116.3 4.8 %gather_fusion.2 = f32[2,8,32,128]{3,2,1,0:T(8,128)} fusion(f32[64,8,32,128]{3,2,1,0:T(8,128)} %convert_element_type.47, s32[1024]{0:T(1024)} %copy-done.18), kind=kCustom, calls=%fused_computation.2 | custom fusion | bytes 524296 | tf_op jit(solution)/shard_map/jit(_take)/gather | solution.py:90
  122.1 2.1 fusion.9
  124.2 2.1 fusion.6
  127.2 35.1 %psum.7 = f32[256,4]{0,1:T(4,128)} all-reduce(f32[256,4]{0,1:T(4,128)S(1)} %fusion.65), channel_id=1, replica_groups=mesh['replica'=32,'tensor'=16] {'tensor'}, use_global_device_ids=true, to_apply=%region_3.4 | all-reduce | flops 1024 | bytes 8192 | tf_op jit(solution)/shard_map/psum | solution.py:129
  164.3 2.1 convolution_convert_fusion
  167.8 1.5 fusion.3
  170.6 83.9 %reduce-scatter.2.cloned.1.call-done = bf16[16,4096]{1,0:T(8,128)(2,1)} async-done(((bf16[256,4096]{1,0:T(8,128)(2,1)}), bf16[16,4096]{1,0:T(8,128)(2,1)}) %reduce-scatter.2.cloned.1.call-update) | async-done | bytes 131088 | tf_op jit(solution)/shard_map/reduce_scatter | solution.py:137
  (104 shorter events, 22.9 us)
Async XLA Ops:
  7.2 157.1 %copy-start = (bf16[256,4096]{1,0:T(8,128)(2,1)S(1)}, bf16[256,4096]{1,0:T(8,128)(2,1)}, u32[]{:S(2)}) copy-start(bf16[256,4096]{1,0:T(8,128)(2,1)} %param.26) | copy-start | bytes 6291460
  7.2 45.9 %copy-start.23 = (s32[64]{0:T(128)S(1)}, s32[64]{0:T(128)}, u32[]{:S(2)}) copy-start(s32[64]{0:T(128)} %param.30) | copy-start | bytes 772
  7.2 46.6 %copy-start.12 = (f32[4,1024]{1,0:T(4,128)S(1)}, f32[4,1024]{1,0:T(4,128)}, u32[]{:S(2)}) copy-start(f32[4,1024]{1,0:T(4,128)} %param.24) | copy-start | bytes 49156
  7.2 102.4 %all-gather.2.cloned.1.call-start = ((), (), s32[]{:S(2)}) async-start(), calls=%async_computation.1 | async-start | bytes 4325376 | tf_op jit(solution)/shard_map/all_gather | solution.py:75
  9.0 245.5 %reduce-scatter.2.cloned.1.call-start = ((), (), s32[]{:S(2)}) async-start(), calls=%async_computation.2 | async-start | bytes 2228224 | tf_op jit(solution)/shard_map/reduce_scatter | solution.py:137
  10.4 2.4 copy-start.20
  10.4 2.4 copy-start.21
  11.5 87.2 %copy-start.4 = (f32[128,8]{1,0:T(8,128)}, f32[128,8]{1,0:T(8,128)S(1)}, u32[]{:S(2)}) copy-start(f32[128,8]{1,0:T(8,128)S(1)} %reduce_window_sum.17) | copy-start | bytes 12292
  13.1 85.6 %copy-start.5 = (f32[128,8]{1,0:T(8,128)}, f32[128,8]{1,0:T(8,128)S(1)}, u32[]{:S(2)}) copy-start(f32[128,8]{1,0:T(8,128)S(1)} %reduce_window_sum.18) | copy-start | bytes 12292
  53.2 2.5 copy-start.16
  53.2 34.4 %copy-start.15 = (pred[2]{0:T(512)(128)(4,1)}, pred[2]{0:T(512)(128)(4,1)S(1)}, u32[]{:S(2)}) copy-start(pred[2]{0:T(512)(128)(4,1)S(1)} %get-tuple-element.4) | copy-start | bytes 10
  53.2 2.5 copy-start.18
  55.1 2.5 copy-start.19
  55.7 31.8 %copy-start.22 = (f32[4,256]{1,0:T(4,128)S(1)}, f32[4,256]{1,0:T(4,128)}, u32[]{:S(2)}) copy-start(f32[4,256]{1,0:T(4,128)} %param.23) | copy-start | bytes 12292
  55.8 31.8 %copy-start.17 = (pred[2]{0:T(512)(128)(4,1)S(1)}, pred[2]{0:T(512)(128)(4,1)}, u32[]{:S(2)}) copy-start(pred[2]{0:T(512)(128)(4,1)} %copy-done.16) | copy-start | bytes 10
  57.6 41.1 %copy-start.8 = (f32[256,8]{0,1:T(8,128)S(1)}, f32[256,8]{0,1:T(8,128)}, u32[]{:S(2)}) copy-start(f32[256,8]{0,1:T(8,128)} %param.19) | copy-start | bytes 24580
  90.4 12.8 %copy-start.3 = (f32[128,256]{0,1:T(8,128)}, f32[128,256]{0,1:T(8,128)S(1)}, u32[]{:S(2)}) copy-start(f32[128,256]{0,1:T(8,128)S(1)} %copy.86) | copy-start | bytes 393220
  98.6 7.6 %copy-start.13 = (s32[8]{0:T(128)}, s32[8]{0:T(128)S(1)}, u32[]{:S(2)}) copy-start(s32[8]{0:T(128)S(1)} %and_select_fusion) | copy-start | bytes 100
  100.6 5.7 %copy-start.6 = (f32[128,4,128]{2,1,0:T(4,128)S(1)}, f32[128,4,128]{2,1,0:T(4,128)}, u32[]{:S(2)}) copy-start(f32[128,4,128]{2,1,0:T(4,128)} %reshape.123) | copy-start | bytes 786436
  102.0 6.0 %copy-start.1 = (f32[128,8,128]{2,1,0:T(8,128)}, f32[128,8,128]{2,1,0:T(8,128)S(1)}, u32[]{:S(2)}) copy-start(f32[128,8,128]{2,1,0:T(8,128)S(1)} %convolution_bitcast_fusion.3) | copy-start | bytes 1572868
  109.6 12.5 %copy-start.10 = (f32[128,8]{0,1:T(8,128)S(1)}, f32[128,8]{0,1:T(8,128)}, u32[]{:S(2)}) copy-start(f32[128,8]{0,1:T(8,128)} %copy.93) | copy-start | bytes 12292
  116.3 8.0 %copy-start.11 = (f32[128,8]{0,1:T(8,128)S(1)}, f32[128,8]{0,1:T(8,128)}, u32[]{:S(2)}) copy-start(f32[128,8]{0,1:T(8,128)} %copy.101) | copy-start | bytes 12292
  116.3 10.8 %copy-start.14 = (s32[8]{0:T(128)S(1)}, s32[8]{0:T(128)}, u32[]{:S(2)}) copy-start(s32[8]{0:T(128)} %copy-done.13) | copy-start | bytes 100
  121.0 5.2 %copy-start.7 = (bf16[256,256]{0,1:T(8,128)(2,1)S(1)}, bf16[256,256]{0,1:T(8,128)(2,1)}, u32[]{:S(2)}) copy-start(bf16[256,256]{0,1:T(8,128)(2,1)} %copy.103) | copy-start | bytes 393220
  (2 other events, 2.7 us)
Sparse Core Ops, SparseCore 0:
  10.1 78.4 all-gather.1
  166.5 87.9 reduce-scatter.1
where the time goes:
time: 262 us; the launch traced here: 261 us
  blocking collectives  100 us (38%)
  waiting for transfers between devices  83.9 us (32%)
  local copies, waits for them, and re-layouts  22.3 us (9%)
  other arithmetic  21.4 us (8%)
  matrix products  18.7 us (7%)
  between operations  14.5 us (6%)
    reduce_scatter x1, waiting for transfers between devices, local(): lax.psum_scatter(jnp.dot(gated, out_weight, preferred_element_type=jnp.fl...  83.9 us
    all_gather x1, blocking collectives, local(): lax.all_gather(cached_tail_bc.astype(jnp.bfloat16), 'replica', axis=0, ti...  37.8 us
    psum x1, blocking collectives, local(): totals = lax.psum(partial_sq, 'tensor')  35.1 us
    all_gather x1, blocking collectives, local(): lax.all_gather(cached_tail_x.astype(jnp.bfloat16), 'replica', axis=0, til...  27.6 us
    gather x3, local copies, waits for them, and re-layouts, local(): taken_rows = jnp.take(piece, position, axis=0)  6.99 us
    convert_element_type x1, other arithmetic, local(): lax.all_gather(cached_states.astype(jnp.bfloat16), 'replica', axis=0, til...  6.65 us
  transfers between devices with their start and end apart: 2, of which 1 were waited for; matrix products, arithmetic and copies ran while one was open for 15% of the time, Pallas kernels for 0%

commit v1 on v0

--- a/solution.py
+++ b/solution.py
@@ -1,3 +1,4 @@
+import functools
 import jax
 import jax.numpy as jnp
 from jax import lax
@@ -9,6 +10,17 @@
 GROUPS = 4
 highest = lax.Precision.HIGHEST
 epsilon = 1e-05
+
+
+def compute_cells_here(body, axis_tag):
+    n_all = lax.axis_size(axis_tag)
+    h_now = body
+    for at in [[(h, h ^ dev) for h in range(n_all)] for dev in (1, 2, 4, 8, 16) if dev < n_all]:
+        h_now = h_now + lax.ppermute(h_now, axis_name=axis_tag, perm=at)
+    return h_now
+
+
+show_regions = functools.partial(compute_cells_here, axis_tag="tensor")
 
 
 def causal_conv(tail_rows, sequence, kernel):
@@ -126,7 +138,7 @@
     by_head = gate_vals.reshape(tokens_dev, local_heads, HEAD_DIM)
     head_squares = jnp.sum(by_head * by_head, axis=2)
     partial_sq = jnp.dot(head_squares, member, precision=highest)
-    totals = lax.psum(partial_sq, "tensor")
+    totals = show_regions(partial_sq)
     mean_sq = jnp.dot(totals, jnp.transpose(member), precision=highest) / (
         HEADS * HEAD_DIM // GROUPS
     )

time: 262 us -> 249 us (0.950)
  blocking collectives: 100 us -> 65.4 us
  starting transfers between devices: 0.08 us -> 15.1 us
  waiting for transfers between devices: 83.9 us -> 93.3 us
    psum x1 -> x0, blocking collectives: 35.1 us -> none  [local(): totals = lax.psum(partial_sq, 'tensor')]
    ppermute x0 -> x4, starting transfers between devices: none -> 15 us  [compute_cells_here(): h_now = h_now + lax.ppermute(h_now, axis_name=axis_tag, perm=at)]
    ppermute x0 -> x4, waiting for transfers between devices: none -> 9.9 us  [compute_cells_here(): h_now = h_now + lax.ppermute(h_now, axis_name=axis_tag, perm=at)]
  transfers between devices with their start and end apart: 2 -> 6, of which waited for: 1 -> 5; matrix products, arithmetic and copies ran while one was open for 15% -> 16% of each run, Pallas kernels for 0% -> 0%
where the time goes in v1:
time: 249 us; the launch traced here: 248 us
  waiting for transfers between devices  93.3 us (37%)
  blocking collectives  65.4 us (26%)
  local copies, waits for them, and re-layouts  22.3 us (9%)
  other arithmetic  19.7 us (8%)
  matrix products  18 us (7%)
  starting transfers between devices  15.1 us (6%)
  between operations  14.6 us (6%)
    reduce_scatter x1, waiting for transfers between devices, local(): lax.psum_scatter(jnp.dot(gated, out_weight, preferred_element_type=jnp.fl...  83.4 us
    all_gather x1, blocking collectives, local(): lax.all_gather(cached_tail_bc.astype(jnp.bfloat16), 'replica', axis=0, ti...  37.9 us
    all_gather x1, blocking collectives, local(): lax.all_gather(cached_tail_x.astype(jnp.bfloat16), 'replica', axis=0, til...  27.5 us
    ppermute x4, starting transfers between devices, compute_cells_here(): h_now = h_now + lax.ppermute(h_now, axis_name=axis_tag, perm=at)  15 us
    ppermute x4, waiting for transfers between devices, compute_cells_here(): h_now = h_now + lax.ppermute(h_now, axis_name=axis_tag, perm=at)  9.9 us
    gather x3, local copies, waits for them, and re-layouts, local(): taken_rows = jnp.take(piece, position, axis=0)  6.99 us
    convert_element_type x1, other arithmetic, local(): lax.all_gather(cached_states.astype(jnp.bfloat16), 'replica', axis=0, til...  6.66 us
  transfers between devices with their start and end apart: 6, of which 5 were waited for; matrix products, arithmetic and copies ran while one was open for 16% of the time, Pallas kernels for 0%

profile of v1, /device:TPU:2, one launch (start us, length us, event | category | flops | bytes accessed | tf_op | source)
XLA Modules:
  0.0 248.4 jit_solution(1251152126528130021)
XLA Ops:
  7.2 1.8 convert_element_type.46
  15.2 37.9 %all_gather.10 = bf16[64,3,1024]{2,1,0:T(4,128)(2,1)S(1)} all-gather(bf16[2,3,1024]{2,1,0:T(4,128)(2,1)S(1)} %copy.87), channel_id=1, replica_groups=mesh['replica'=32,'tensor'=16] {'replica'}, dimensions={0}, use_global_device_ids=true | all-gather | bytes 405504 | tf_op jit(solution)/shard_map/all_gather | solution.py:93
  57.7 27.5 %all_gather.9 = bf16[64,3,256]{2,1,0:T(4,128)(2,1)S(1)} all-gather(bf16[2,3,256]{2,1,0:T(4,128)(2,1)S(1)} %copy.85), channel_id=1, replica_groups=mesh['replica'=32,'tensor'=16] {'replica'}, dimensions={0}, use_global_device_ids=true | all-gather | bytes 101376 | tf_op jit(solution)/shard_map/all_gather | solution.py:90
  85.9 1.6 gather_fusion
  93.1 1.5 copy.93
  95.4 1.5 copy.101
  97.0 1.7 copy.103
  103.3 1.6 convolution_bitcast_fusion.7
  108.0 1.6 convolution_bitcast_fusion.5
  109.6 6.7 %convert_element_type.47 = f32[64,8,32,128]{3,2,1,0:T(8,128)} convert(bf16[64,8,32,128]{3,2,1,0:T(8,128)(2,1)} %all-gather.2.cloned.1.call-done) | non-fusion elementwise | flops 2097152 | bytes 12582912 | tf_op jit(solution)/shard_map/convert_element_type | solution.py:87
  116.2 4.8 %gather_fusion.2 = f32[2,8,32,128]{3,2,1,0:T(8,128)} fusion(f32[64,8,32,128]{3,2,1,0:T(8,128)} %convert_element_type.47, s32[1024]{0:T(1024)} %copy-done.18), kind=kCustom, calls=%fused_computation.2 | custom fusion | bytes 524296 | tf_op jit(solution)/shard_map/jit(_take)/gather | solution.py:102
  122.1 2.1 fusion.9
  124.2 2.1 fusion.6
  126.5 3.6 %collective-permute-start = (f32[256,4]{0,1:T(4,128)S(1)}, f32[256,4]{0,1:T(4,128)S(1)}, u32[]{:S(2)}, u32[]{:S(2)}) collective-permute-start(f32[256,4]{0,1:T(4,128)S(1)} %fusion.66), channel_id=1, source_target_pairs={{0,1},{1,0},{2,3},{3,2},{4,5},{5,4},{6,7},{7,6},{8,9},{9,8},{10,11... | collective-permute-start | bytes 12296 | tf_op jit(solution)/shard_map/ppermute | solution.py:19
  130.1 1.9 collective-permute-done
  132.0 5.1 %collective-permute-start.1 = (f32[256,4]{0,1:T(4,128)S(1)}, f32[256,4]{0,1:T(4,128)S(1)}, u32[]{:S(2)}, u32[]{:S(2)}) collective-permute-start(f32[256,4]{0,1:T(4,128)S(1)} %add.169), channel_id=1, source_target_pairs={{0,2},{1,3},{2,0},{3,1},{4,6},{5,7},{6,4},{7,5},{8,10},{9,11},{10,... | collective-permute-start | bytes 12296 | tf_op jit(solution)/shard_map/ppermute | solution.py:19
  137.1 1.9 collective-permute-done.1
  139.0 2.4 collective-permute-start.2
  141.4 3.1 %collective-permute-done.2 = f32[256,4]{0,1:T(4,128)S(1)} collective-permute-done((f32[256,4]{0,1:T(4,128)S(1)}, f32[256,4]{0,1:T(4,128)S(1)}, u32[]{:S(2)}, u32[]{:S(2)}) %collective-permute-start.2) | collective-permute-done | bytes 4128 | tf_op jit(solution)/shard_map/ppermute | solution.py:19
  144.5 4.0 %collective-permute-start.3 = (f32[256,4]{0,1:T(4,128)S(1)}, f32[256,4]{0,1:T(4,128)S(1)}, u32[]{:S(2)}, u32[]{:S(2)}) collective-permute-start(f32[256,4]{0,1:T(4,128)S(1)} %add.171), channel_id=1, source_target_pairs={{0,8},{1,9},{2,10},{3,11},{4,12},{5,13},{6,14},{7,15},{8,0},{9,1},... | collective-permute-start | bytes 12296 | tf_op jit(solution)/shard_map/ppermute | solution.py:19
  148.5 3.0 %collective-permute-done.3 = f32[256,4]{0,1:T(4,128)S(1)} collective-permute-done((f32[256,4]{0,1:T(4,128)S(1)}, f32[256,4]{0,1:T(4,128)S(1)}, u32[]{:S(2)}, u32[]{:S(2)}) %collective-permute-start.3) | collective-permute-done | bytes 4128 | tf_op jit(solution)/shard_map/ppermute | solution.py:19
  151.8 2.1 convolution_convert_fusion
  155.3 1.5 fusion.3
  158.2 83.4 %reduce-scatter.2.cloned.1.call-done = bf16[16,4096]{1,0:T(8,128)(2,1)} async-done(((bf16[256,4096]{1,0:T(8,128)(2,1)}), bf16[16,4096]{1,0:T(8,128)(2,1)}) %reduce-scatter.2.cloned.1.call-update) | async-done | bytes 131088 | tf_op jit(solution)/shard_map/reduce_scatter | solution.py:149
  (118 shorter events, 29.7 us)
Async XLA Ops:
  7.2 144.7 %copy-start = (bf16[256,4096]{1,0:T(8,128)(2,1)S(1)}, bf16[256,4096]{1,0:T(8,128)(2,1)}, u32[]{:S(2)}) copy-start(bf16[256,4096]{1,0:T(8,128)(2,1)} %param.26) | copy-start | bytes 6291460
  7.2 46.0 %copy-start.25 = (s32[64]{0:T(128)S(1)}, s32[64]{0:T(128)}, u32[]{:S(2)}) copy-start(s32[64]{0:T(128)} %param.30) | copy-start | bytes 772
  7.2 46.7 %copy-start.12 = (f32[4,1024]{1,0:T(4,128)S(1)}, f32[4,1024]{1,0:T(4,128)}, u32[]{:S(2)}) copy-start(f32[4,1024]{1,0:T(4,128)} %param.24) | copy-start | bytes 49156
  7.2 102.4 %all-gather.2.cloned.1.call-start = ((), (), s32[]{:S(2)}) async-start(), calls=%async_computation.1 | async-start | bytes 4325376 | tf_op jit(solution)/shard_map/all_gather | solution.py:87
  9.0 232.5 %reduce-scatter.2.cloned.1.call-start = ((), (), s32[]{:S(2)}) async-start(), calls=%async_computation.2 | async-start | bytes 2228224 | tf_op jit(solution)/shard_map/reduce_scatter | solution.py:149
  11.5 87.1 %copy-start.4 = (f32[128,8]{1,0:T(8,128)}, f32[128,8]{1,0:T(8,128)S(1)}, u32[]{:S(2)}) copy-start(f32[128,8]{1,0:T(8,128)S(1)} %reduce_window_sum.17) | copy-start | bytes 12292
  13.1 85.6 %copy-start.5 = (f32[128,8]{1,0:T(8,128)}, f32[128,8]{1,0:T(8,128)S(1)}, u32[]{:S(2)}) copy-start(f32[128,8]{1,0:T(8,128)S(1)} %reduce_window_sum.18) | copy-start | bytes 12292
  53.3 34.3 %copy-start.15 = (pred[2]{0:T(512)(128)(4,1)}, pred[2]{0:T(512)(128)(4,1)S(1)}, u32[]{:S(2)}) copy-start(pred[2]{0:T(512)(128)(4,1)S(1)} %get-tuple-element.4) | copy-start | bytes 10
  55.8 31.8 %copy-start.22 = (f32[4,256]{1,0:T(4,128)S(1)}, f32[4,256]{1,0:T(4,128)}, u32[]{:S(2)}) copy-start(f32[4,256]{1,0:T(4,128)} %param.23) | copy-start | bytes 12292
  55.8 31.8 %copy-start.17 = (pred[2]{0:T(512)(128)(4,1)S(1)}, pred[2]{0:T(512)(128)(4,1)}, u32[]{:S(2)}) copy-start(pred[2]{0:T(512)(128)(4,1)} %copy-done.16) | copy-start | bytes 10
  57.7 41.0 %copy-start.8 = (f32[256,8]{0,1:T(8,128)S(1)}, f32[256,8]{0,1:T(8,128)}, u32[]{:S(2)}) copy-start(f32[256,8]{0,1:T(8,128)} %param.19) | copy-start | bytes 24580
  90.4 12.8 %copy-start.3 = (f32[128,256]{0,1:T(8,128)}, f32[128,256]{0,1:T(8,128)S(1)}, u32[]{:S(2)}) copy-start(f32[128,256]{0,1:T(8,128)S(1)} %copy.86) | copy-start | bytes 393220
  98.6 7.6 %copy-start.13 = (s32[8]{0:T(128)}, s32[8]{0:T(128)S(1)}, u32[]{:S(2)}) copy-start(s32[8]{0:T(128)S(1)} %and_select_fusion) | copy-start | bytes 100
  100.5 5.7 %copy-start.6 = (f32[128,4,128]{2,1,0:T(4,128)S(1)}, f32[128,4,128]{2,1,0:T(4,128)}, u32[]{:S(2)}) copy-start(f32[128,4,128]{2,1,0:T(4,128)} %reshape.123) | copy-start | bytes 786436
  102.0 6.0 %copy-start.1 = (f32[128,8,128]{2,1,0:T(8,128)}, f32[128,8,128]{2,1,0:T(8,128)S(1)}, u32[]{:S(2)}) copy-start(f32[128,8,128]{2,1,0:T(8,128)S(1)} %convolution_bitcast_fusion.3) | copy-start | bytes 1572868
  109.6 12.5 %copy-start.10 = (f32[128,8]{0,1:T(8,128)S(1)}, f32[128,8]{0,1:T(8,128)}, u32[]{:S(2)}) copy-start(f32[128,8]{0,1:T(8,128)} %copy.93) | copy-start | bytes 12292
  116.2 8.0 %copy-start.11 = (f32[128,8]{0,1:T(8,128)S(1)}, f32[128,8]{0,1:T(8,128)}, u32[]{:S(2)}) copy-start(f32[128,8]{0,1:T(8,128)} %copy.101) | copy-start | bytes 12292
  116.2 10.1 %copy-start.14 = (s32[8]{0:T(128)S(1)}, s32[8]{0:T(128)}, u32[]{:S(2)}) copy-start(s32[8]{0:T(128)} %copy-done.13) | copy-start | bytes 100
  121.0 30.7 %copy-start.23 = (f32[256]{0:T(256)S(1)}, f32[256]{0:T(256)}, u32[]{:S(2)}) copy-start(f32[256]{0:T(256)} %param.25) | copy-start | bytes 3076
  121.0 30.7 %copy-start.24 = (pred[256]{0:T(512)(128)(4,1)S(1)}, pred[256]{0:T(512)(128)(4,1)}, u32[]{:S(2)}) copy-start(pred[256]{0:T(512)(128)(4,1)} %get-tuple-element.38) | copy-start | bytes 772
  126.5 5.5 %collective-permute-start = (f32[256,4]{0,1:T(4,128)S(1)}, f32[256,4]{0,1:T(4,128)S(1)}, u32[]{:S(2)}, u32[]{:S(2)}) collective-permute-start(f32[256,4]{0,1:T(4,128)S(1)} %fusion.66), channel_id=1, source_target_pairs={{0,1},{1,0},{2,3},{3,2},{4,5},{5,4},{6,7},{7,6},{8,9},{9,8},{10,11... | collective-permute-start | bytes 12296 | tf_op jit(solution)/shard_map/ppermute | solution.py:19
  132.0 7.0 %collective-permute-start.1 = (f32[256,4]{0,1:T(4,128)S(1)}, f32[256,4]{0,1:T(4,128)S(1)}, u32[]{:S(2)}, u32[]{:S(2)}) collective-permute-start(f32[256,4]{0,1:T(4,128)S(1)} %add.169), channel_id=1, source_target_pairs={{0,2},{1,3},{2,0},{3,1},{4,6},{5,7},{6,4},{7,5},{8,10},{9,11},{10,... | collective-permute-start | bytes 12296 | tf_op jit(solution)/shard_map/ppermute | solution.py:19
  139.0 5.5 %collective-permute-start.2 = (f32[256,4]{0,1:T(4,128)S(1)}, f32[256,4]{0,1:T(4,128)S(1)}, u32[]{:S(2)}, u32[]{:S(2)}) collective-permute-start(f32[256,4]{0,1:T(4,128)S(1)} %add.170), channel_id=1, source_target_pairs={{0,4},{1,5},{2,6},{3,7},{4,0},{5,1},{6,2},{7,3},{8,12},{9,13},{10,... | collective-permute-start | bytes 12296 | tf_op jit(solution)/shard_map/ppermute | solution.py:19
  144.5 7.0 %collective-permute-start.3 = (f32[256,4]{0,1:T(4,128)S(1)}, f32[256,4]{0,1:T(4,128)S(1)}, u32[]{:S(2)}, u32[]{:S(2)}) collective-permute-start(f32[256,4]{0,1:T(4,128)S(1)} %add.171), channel_id=1, source_target_pairs={{0,8},{1,9},{2,10},{3,11},{4,12},{5,13},{6,14},{7,15},{8,0},{9,1},... | collective-permute-start | bytes 12296 | tf_op jit(solution)/shard_map/ppermute | solution.py:19
  (8 other events, 20.4 us)
Sparse Core Ops, SparseCore 0:
  10.1 78.5 all-gather.1
  154.1 87.4 reduce-scatter.1
